TPU v7x, 32 devices: a whole 2x2x4 slice. The times are simulated.
32 devices in a mesh: groups: 2 (over x), ctx: 16 (over z, y, core).
Axes of the slice: x: 2, y: 2, z: 4, core: 2. Of those that a mesh axis runs over, the one named last changes fastest.
Arguments:
- residual: bfloat16 [4096, 2048], P(('groups', 'ctx')), parts along dimension 0, may hold values from -200 to 200
- queries: bfloat16 [4096, 2048], P(('groups', 'ctx')), parts along dimension 0, may hold values from -64 to 64
- keys: bfloat16 [4096, 256], P(('groups', 'ctx')), parts along dimension 0, may hold values from -64 to 64
- values: bfloat16 [4096, 256], P(('groups', 'ctx')), parts along dimension 0, may hold values from -6 to 6
- block_order: int32 [32], P('groups'), parts along dimension 0, may hold values from 0 to 3, as said below
- routes: int32 [4096, 8], P(('groups', 'ctx')), parts along dimension 0, may hold values from 0 to 15, as said below
- route_weights: float32 [4096, 8], P(('groups', 'ctx')), parts along dimension 0, may hold values from 0.1 to 1
- out_weight: bfloat16 [2048, 2048], P(None, 'ctx'), may hold values from -0.125 to 0.125
- norm_gain: float32 [2048], replicated, may hold values from 0.5 to 1.5
- w_gate_up: bfloat16 [16, 2048, 1536], P('ctx'), may hold values from -0.125 to 0.125
- w_down: bfloat16 [16, 768, 2048], P('ctx'), may hold values from -0.21875 to 0.21875
Outputs:
- context: bfloat16 [4096, 2048], P(('groups', 'ctx')), parts along dimension 0
- mixed: bfloat16 [4096, 2048], P(('groups', 'ctx')), parts along dimension 0
There are 2 independent parts, one for each index of `groups`. A program takes and returns all parts, laid end to end along the dimension named above; an argument that names none is the same for every part. Nothing has to cross between parts.
Inputs may be any that keep to these rules, and one draw needn't show every extreme that they name: `block_order`: for each i below 4, the entries at the indices congruent to i modulo 4 hold every number from 0 to 3 once. `routes`: each token names 8 different experts. Among the tokens of one device no expert is named more than 72 times, and some expert is named exactly 72 times by the tokens of every device.
All inputs are finite; a program needn't handle non-finite values.
Results may differ from a plain program's by a relative error of at most 0.005.
Values may be sent and summed in bfloat16 or wider, within the bound.
No kernel may reach another device: no remote copies, remote signals or barrier semaphores. Data moves between devices by JAX's collectives and lax.ppermute only.
A program may use at most 128 MiB of HBM per device.

v0:
```python
import jax
import jax.numpy as jnp
from jax import lax
from jax.sharding import PartitionSpec as P

D = 2048
HEAD_SIZE = 128
FF = 768
QUERY_HEADS = 16
KEY_VALUE_HEADS = 2
TOPK = 8
SEQS = 4


def shifted(array, axis, by):
    devices = lax.axis_size(axis)
    return lax.ppermute(array, axis, [(i, (i + by) % devices) for i in range(devices)])


def local(
    residual,
    queries,
    keys,
    values,
    block_order,
    routes,
    route_weights,
    out_weight,
    norm_gain,
    w_gate_up,
    w_down,
):
    device_row_count = queries.shape[0]
    query_group_width = QUERY_HEADS // KEY_VALUE_HEADS
    devices = lax.axis_size("ctx")
    cycle_length = devices // SEQS
    own_index = lax.axis_index("ctx")
    full_weight = lax.all_gather(out_weight, "ctx", axis=1, tiled=True)
    query_position = block_order[own_index]
    query_head_rows = (
        queries.reshape(device_row_count, KEY_VALUE_HEADS, query_group_width, HEAD_SIZE)
        .transpose(1, 2, 0, 3)
        .reshape(KEY_VALUE_HEADS, query_group_width * device_row_count, HEAD_SIZE)
    )
    query_offset = jnp.arange(query_group_width * device_row_count) % device_row_count
    key_offset = jnp.arange(device_row_count)
    scale = HEAD_SIZE ** (-0.5)

    def update(carry, key_value_tuple, key_position):
        summed, running_max, totals = carry
        local_key_block = key_value_tuple[0].reshape(device_row_count, KEY_VALUE_HEADS, HEAD_SIZE)
        local_value_block = key_value_tuple[1].reshape(device_row_count, KEY_VALUE_HEADS, HEAD_SIZE)
        scores = (
            jnp.einsum(
                "hqd,khd->hqk", query_head_rows, local_key_block, preferred_element_type=jnp.float32
            )
            * scale
        )
        visible = (
            key_position * device_row_count + key_offset[None, :]
            <= query_position * device_row_count + query_offset[:, None]
        )
        scores = jnp.where(visible[None], scores, -jnp.inf)
        new_max = jnp.maximum(running_max, jnp.max(scores, axis=-1))
        factor = jnp.exp(running_max - new_max)
        weights = jnp.exp(scores - new_max[..., None])
        totals = totals * factor + jnp.sum(weights, axis=-1)
        summed = summed * factor[..., None] + jnp.einsum(
            "hqk,khd->hqd",
            weights.astype(jnp.bfloat16),
            local_value_block,
            preferred_element_type=jnp.float32,
        )
        return (summed, new_max, totals)

    initial = (
        jnp.zeros((KEY_VALUE_HEADS, query_group_width * device_row_count, HEAD_SIZE), jnp.float32),
        jnp.full((KEY_VALUE_HEADS, query_group_width * device_row_count), -jnp.inf, jnp.float32),
        jnp.zeros((KEY_VALUE_HEADS, query_group_width * device_row_count), jnp.float32),
    )
    local_pair = jnp.stack([keys, values])
    carry = update(initial, local_pair, query_position)

    def advance(step, state):
        current, moving = state
        moving = shifted(moving, "ctx", SEQS)
        anchor = jnp.mod(own_index - SEQS * step, devices)
        key_position = block_order[anchor]
        current = lax.cond(
            key_position <= query_position,
            lambda inner: update(inner, moving, key_position),
            lambda inner: inner,
            current,
        )
        return (current, moving)

    carry, passed = lax.fori_loop(1, cycle_length, advance, (carry, local_pair))
    summed, running_max, totals = carry
    context = (
        (summed / totals[..., None])
        .reshape(KEY_VALUE_HEADS, query_group_width, device_row_count, HEAD_SIZE)
        .transpose(2, 0, 1, 3)
        .reshape(device_row_count, QUERY_HEADS * HEAD_SIZE)
        .astype(jnp.bfloat16)
    )
    projected = jnp.dot(context, full_weight, preferred_element_type=jnp.float32)
    updated = residual.astype(jnp.float32) + projected
    normed = (
        updated * lax.rsqrt(jnp.mean(updated * updated, axis=-1, keepdims=True) + 1e-06) * norm_gain
    ).astype(jnp.bfloat16)
    experts = devices * w_gate_up.shape[0]
    capacity = 9 * device_row_count * TOPK // (8 * experts)
    expert_ids = routes.reshape(-1)
    one_hot = (expert_ids[:, None] == jnp.arange(experts, dtype=jnp.int32)[None, :]).astype(
        jnp.int32
    )
    ranks = jnp.sum(jnp.cumsum(one_hot, axis=0) * one_hot, axis=1) - 1
    target = expert_ids * capacity + ranks
    source_row = jnp.arange(device_row_count * TOPK) // TOPK
    outgoing = (
        jnp.zeros((experts * capacity, D), jnp.bfloat16)
        .at[target]
        .set(normed[source_row])
        .reshape(experts, capacity, D)
    )
    arrived = lax.all_to_all(outgoing, "ctx", split_axis=0, concat_axis=0, tiled=True)
    flat = arrived.reshape(-1, D)
    both = jnp.dot(flat, w_gate_up[0], preferred_element_type=jnp.float32)
    hidden = (jax.nn.silu(both[:, :FF]) * both[:, FF:]).astype(jnp.bfloat16)
    result = (
        jnp.dot(hidden, w_down[0], preferred_element_type=jnp.float32)
        .astype(jnp.bfloat16)
        .reshape(arrived.shape)
    )
    returned = lax.all_to_all(result, "ctx", split_axis=0, concat_axis=0, tiled=True)
    gathered = returned.reshape(-1, D)[target].reshape(device_row_count, TOPK, D)
    gates = route_weights / jnp.sum(route_weights, axis=-1, keepdims=True)
    mixed = updated
    for slot in range(TOPK):
        mixed = mixed + gates[:, slot : slot + 1] * gathered[:, slot].astype(jnp.float32)
    return (context, mixed.astype(jnp.bfloat16))


def solution(mesh):
    placed = (
        P(("groups", "ctx"), None),
        P(("groups", "ctx"), None),
        P(("groups", "ctx"), None),
        P(("groups", "ctx"), None),
        P("groups"),
        P(("groups", "ctx"), None),
        P(("groups", "ctx"), None),
        P(None, "ctx"),
        P(),
        P("ctx", None, None),
        P("ctx", None, None),
    )
    return jax.shard_map(
        local,
        mesh=mesh,
        in_specs=placed,
        out_specs=(P(("groups", "ctx"), None), P(("groups", "ctx"), None)),
        check_vma=False,
    )
```

profile of v0, /device:TPU:13, one launch (start us, length us, event | category | flops | bytes accessed | tf_op | source)
XLA Modules:
  0.0 407.0 jit_solution(8898957640358070973)
XLA Ops:
  7.2 0.0 copy-start
  7.2 0.0 all-gather.2.cloned.1.call-start
  7.2 0.7 all-gather.2.cloned.1.call-update
  7.9 0.9 copy.32
  8.9 0.1 eq.39
  9.0 0.1 eq.35
  9.1 1.1 copy.58
  10.2 0.9 copy.24
  11.1 0.9 copy.28
  12.1 1.0 copy.29
  13.1 1.3 dynamic_slice.13
  15.1 0.7 pad_maximum_fusion
  15.8 0.1 broadcast_compare_fusion.1
  15.9 1.4 fusion.49
  17.3 0.2 fusion.29
  17.5 1.6 convolution_add_fusion.2
  19.1 40.9 %while.22 = (s32[]{:T(128)}, f32[2,1024,128]{2,1,0:T(8,128)}, f32[2,1024]{1,0:T(2,128)S(1)}, f32[2,1024]{1,0:T(2,128)S(1)}, bf16[2,128,256]{1,2,0:T(8,128)(2,1)S...) while((s32[]{:T(128)}, f32[2,1024,128]{2,1,0:T(8,128)}, ...), condition=%wide.region_7.8_spmd.clone, body=%wide.region_2.7_spmd.clone.sunk | while | flops 136719504 | bytes 7379506 | solution.py:97
  19.1 1.3 collective-permute-start
  20.4 0.6 dynamic_slice.16
  22.4 6.5 %collective-permute-done = bf16[2,128,256]{1,2,0:T(8,128)(2,1)S(1)} collective-permute-done((bf16[2,128,256]{1,2,0:T(8,128)(2,1)S(1)}, bf16[2,128,256]{1,2,0:T(8,128)(2,1)S(1)}, u32[]{:S(2)}, u32[]{:S(2)}) %collective-permute-start) | collective-permute-done | bytes 131104 | tf_op jit(solution)/shard_map/while/body/eval_jaxpr/ppermute | solution.py:17
  28.9 6.0 %conditional.3 = ((f32[2,1024,128]{2,1,0:T(8,128)}, f32[2,1024]{1,0:T(2,128)S(1)}, f32[2,1024]{1,0:T(2,128)S(1)})) conditional(s32[]{:T(128)} %convert_element_type.146, (f32[2,1024,128]{2,1,0:T(8,128)}, f32[2,1024]{1,0:T(2,128)S(1)}, f32[2,1024]{1,0:T(2,128)S(1)}) %tuple.77, (s32[]{:T(128)}, s32[128]{0:T(128)S(1)}, s32[]{:T(128)}, ...), branch_computations={%region_3.3_spmd, %region_4.6_spmd.clone} | conditional | flops 136718464 | bytes 6583872 | solution.py:89
  30.3 0.1 broadcast_compare_fusion
  30.4 1.5 fusion.47
  31.9 0.2 fusion.5
  32.1 2.8 convolution_add_fusion
  34.9 0.1 collective-permute-start
  35.0 0.6 dynamic_slice.16
  36.9 6.1 %collective-permute-done = bf16[2,128,256]{1,2,0:T(8,128)(2,1)S(1)} collective-permute-done((bf16[2,128,256]{1,2,0:T(8,128)(2,1)S(1)}, bf16[2,128,256]{1,2,0:T(8,128)(2,1)S(1)}, u32[]{:S(2)}, u32[]{:S(2)}) %collective-permute-start) | collective-permute-done | bytes 131104 | tf_op jit(solution)/shard_map/while/body/eval_jaxpr/ppermute | solution.py:17
  43.1 6.0 %conditional.3 = ((f32[2,1024,128]{2,1,0:T(8,128)}, f32[2,1024]{1,0:T(2,128)S(1)}, f32[2,1024]{1,0:T(2,128)S(1)})) conditional(s32[]{:T(128)} %convert_element_type.146, (f32[2,1024,128]{2,1,0:T(8,128)}, f32[2,1024]{1,0:T(2,128)S(1)}, f32[2,1024]{1,0:T(2,128)S(1)}) %tuple.77, (s32[]{:T(128)}, s32[128]{0:T(128)S(1)}, s32[]{:T(128)}, ...), branch_computations={%region_3.3_spmd, %region_4.6_spmd.clone} | conditional | flops 136718464 | bytes 6583872 | solution.py:89
  44.4 0.1 broadcast_compare_fusion
  44.6 1.4 fusion.47
  46.1 0.2 fusion.5
  46.2 2.8 convolution_add_fusion
  49.1 0.1 collective-permute-start
  49.2 0.6 dynamic_slice.16
  51.1 2.8 collective-permute-done
  53.9 6.0 %conditional.3 = ((f32[2,1024,128]{2,1,0:T(8,128)}, f32[2,1024]{1,0:T(2,128)S(1)}, f32[2,1024]{1,0:T(2,128)S(1)})) conditional(s32[]{:T(128)} %convert_element_type.146, (f32[2,1024,128]{2,1,0:T(8,128)}, f32[2,1024]{1,0:T(2,128)S(1)}, f32[2,1024]{1,0:T(2,128)S(1)}) %tuple.77, (s32[]{:T(128)}, s32[128]{0:T(128)S(1)}, s32[]{:T(128)}, ...), branch_computations={%region_3.3_spmd, %region_4.6_spmd.clone} | conditional | flops 136718464 | bytes 6583872 | solution.py:89
  55.3 0.1 broadcast_compare_fusion
  55.4 1.5 fusion.47
  56.9 0.2 fusion.5
  57.1 2.8 convolution_add_fusion
  60.0 1.6 divide_convert_fusion
  61.5 0.3 copy.30
  61.9 0.9 copy.97
  62.8 4.5 %reduce-window.6 = s32[16,8,128]{2,1,0:T(8,128)S(1)} reduce-window(s32[16,8,128]{2,1,0:T(8,128)S(1)} %fusion.39, s32[]{:T(128)} %constant.121.clone.1), window={size=1x1x128 pad=0_0x0_0x127_0}, to_apply=%region_9.10 | reduce-window | flops 2080768 | bytes 131076 | tf_op jit(solution)/shard_map/reduce-window
  67.3 0.1 slice.92
  67.4 0.1 copy.34
  67.6 0.1 copy.35
  67.7 0.1 copy.31
  67.8 0.1 mul.174
  67.9 0.1 broadcast_add_fusion.1
  68.1 25.8 %all-gather.2.cloned.1.call-done = bf16[2048,2048]{1,0:T(8,128)(2,1)} async-done(((bf16[2048,128]{1,0:T(8,128)(2,1)}), bf16[2048,2048]{1,0:T(8,128)(2,1)}) %all-gather.2.cloned.1.call-update) | async-done | bytes 8388624 | tf_op jit(solution)/shard_map/all_gather | solution.py:38
  93.8 5.0 %multiply_reduce_fusion = (f32[128]{0:T(128)S(1)}, f32[128,2048]{1,0:T(8,128)S(1)}) fusion(bf16[128,2048]{1,0:T(8,128)(2,1)} %bitcast.138, bf16[2048,2048]{1,0:T(8,128)(2,1)} %all-gather.2.cloned.1.call-done, bf16[128,2048]{1,0:T(8,128)(2,1)} %param.15), kind=kOutput, calls=%fused_computation.52 | convolution fusion | flops 1074790272 | bytes 10486272 | tf_op jit(solution)/shard_map/dot_general | solution.py:106
  98.8 1.0 copy-done.2
  99.8 0.9 multiply_convert_fusion
  100.7 23.8 %scatter_custom_fusion = bf16[1152,2048]{1,0:T(8,128)(2,1)} fusion(s32[1024]{0:T(1024)S(1)} %bitcast.148, bf16[128,2048]{1,0:T(8,128)(2,1)} %multiply_convert_fusion, s32[1024]{0:T(1024)S(1)} %broadcast_clamp_fusion.1, bf16[]{:T(256)} %constant.129.clone.1), kind=kCustom, calls=%fused_computation.23 | custom fusion | bytes 4719104 | tf_op jit(solution)/shard_map/scatter | solution.py:123
  124.5 112.1 %all_to_all.10 = bf16[16,72,2048]{2,1,0:T(8,128)(2,1)S(1)} all-to-all(bf16[16,72,2048]{2,1,0:T(8,128)(2,1)} %bitcast.133), channel_id=1, replica_groups=mesh['groups'=2,'ctx'=16] {'ctx'}, dimensions={0} | all-to-all | bytes 9437184 | tf_op jit(solution)/shard_map/all_to_all | solution.py:126
  236.6 9.7 %fusion.10 = f32[1152,1536]{1,0:T(8,128)S(1)} fusion(bf16[1152,2048]{1,0:T(8,128)(2,1)S(1)} %bitcast.137, bf16[1,2048,1536]{2,1,0:T(8,128)(2,1)} %param.24), kind=kOutput, calls=%fused_computation.21 | convolution fusion | flops 7247757312 | bytes 18087936 | tf_op jit(solution)/shard_map/dot_general | solution.py:128
  246.3 5.7 %convolution_convert_fusion = bf16[1152,2048]{1,0:T(8,128)(2,1)} fusion(bf16[1,768,2048]{2,1,0:T(8,128)(2,1)S(1)} %copy-done, f32[1152,1536]{1,0:T(8,128)S(1)} %fusion.10), kind=kOutput, calls=%fused_computation.20 | convolution fusion | flops 3631546368 | bytes 14942208 | tf_op jit(solution)/shard_map/dot_general | solution.py:131
  251.9 4.9 %all-to-all-start.1 = ((bf16[16,72,2048]{2,1,0:T(8,128)(2,1)}), bf16[16,72,2048]{2,1,0:T(8,128)(2,1)}, u32[]{:S(2)}, u32[]{:S(2)}) async-start(bf16[16,72,2048]{2,1,0:T(8,128)(2,1)} %bitcast.136), calls=%async_computation.1 | async-start | bytes 9437184 | tf_op jit(solution)/shard_map/all_to_all | solution.py:135
  256.9 103.6 %all-to-all-done.1 = bf16[16,72,2048]{2,1,0:T(8,128)(2,1)} async-done(((bf16[16,72,2048]{2,1,0:T(8,128)(2,1)}), bf16[16,72,2048]{2,1,0:T(8,128)(2,1)}, u32[]{:S(2)}, u32[]{:S(2)}) %all-to-all-start.1) | async-done | bytes 4718624 | tf_op jit(solution)/shard_map/all_to_all | solution.py:135
  360.6 11.8 %gather_fusion = bf16[1024,2048]{1,0:T(8,128)(2,1)} fusion(bf16[1152,2048]{1,0:T(8,128)(2,1)} %bitcast.20, s32[1024]{0:T(1024)S(1)} %broadcast_clamp_fusion), kind=kCustom, calls=%fused_computation.1 | custom fusion | bytes 8392704 | tf_op jit(solution)/shard_map/gather | solution.py:136
  372.4 22.3 %fusion.48 = (bf16[128,1,2048]{2,1,0:T(2,128)(2,1)S(1)}, bf16[128,1,2048]{2,1,0:T(2,128)(2,1)S(1)}, bf16[128,1,2048]{2,1,0:T(2,128)(2,1)S(1)}, bf16[128,1,2048]{...) fusion(bf16[128,8,2048]{2,1,0:T(8,128)(2,1)} %bitcast.130), kind=kLoop, calls=%fused_computation.112 | loop fusion | bytes 8388608 | tf_op jit(solution)/shard_map/slice | solution.py:140
  394.7 5.5 %fusion.21 = bf16[128,2048]{1,0:T(8,128)(2,1)} fusion(f32[128,2048]{1,0:T(8,128)S(1)} %copy-done.3, bf16[128,1,2048]{2,1,0:T(2,128)(2,1)S(1)} %get-tuple-element.415, bf16[128,1,2048]{2,1,0:T(2,128)(2,1)S(1)} %get-tuple-element.409, bf16[128,1,2048]{2,1,0:T(2,128)(2,1)S(1)} %get-tuple-element.410, bf16[128,1,2048]{2,1,0:T(2,128)(2,1)S(1)} %get-tuple-element.411, ...), kind=kLoop, calls=%fused_computation.36 | loop fusion | flops 6553600 | bytes 5771264 | tf_op jit(solution)/shard_map/convert_element_type | solution.py:141
  (65 shorter events, 0.4 us)
Async XLA Ops:
  7.2 239.1 %copy-start = (bf16[1,768,2048]{2,1,0:T(8,128)(2,1)S(1)}, bf16[1,768,2048]{2,1,0:T(8,128)(2,1)}, u32[]{:S(2)}) copy-start(bf16[1,768,2048]{2,1,0:T(8,128)(2,1)} %param.25) | copy-start | bytes 9437188
  7.2 10.3 %copy-start.4 = (bf16[128,256]{1,0:T(8,128)(2,1)S(1)}, bf16[128,256]{1,0:T(8,128)(2,1)}, u32[]{:S(2)}) copy-start(bf16[128,256]{1,0:T(8,128)(2,1)} %param.18) | copy-start | bytes 196612
  7.2 11.9 %copy-start.9 = (s32[16]{0:T(128)S(1)}, s32[16]{0:T(128)}, u32[]{:S(2)}) copy-start(s32[16]{0:T(128)} %param.19) | copy-start | bytes 196
  7.2 86.6 %all-gather.2.cloned.1.call-start = ((), (), s32[]{:S(2)}) async-start(), calls=%async_computation.2 | async-start | bytes 8912896 | tf_op jit(solution)/shard_map/all_gather | solution.py:38
  15.7 3.3 copy-start.5
  19.1 48.6 %copy-start.6 = (s32[128,8]{0,1:T(8,128)S(1)}, s32[128,8]{0,1:T(8,128)}, u32[]{:S(2)}) copy-start(s32[128,8]{0,1:T(8,128)} %param.20) | copy-start | bytes 12292
  19.1 9.8 %collective-permute-start = (bf16[2,128,256]{1,2,0:T(8,128)(2,1)S(1)}, bf16[2,128,256]{1,2,0:T(8,128)(2,1)S(1)}, u32[]{:S(2)}, u32[]{:S(2)}) collective-permute-start(bf16[2,128,256]{1,2,0:T(8,128)(2,1)S(1)} %get-tuple-element.515), channel_id=1, source_target_pairs={{0,4},{1,5},{2,6},{3,7},{4,8},{5,9},{6,10},{7,11},{8,12},{9,13},{1... | collective-permute-start | bytes 393224 | tf_op jit(solution)/shard_map/while/body/eval_jaxpr/ppermute | solution.py:17
  34.9 8.1 %collective-permute-start = (bf16[2,128,256]{1,2,0:T(8,128)(2,1)S(1)}, bf16[2,128,256]{1,2,0:T(8,128)(2,1)S(1)}, u32[]{:S(2)}, u32[]{:S(2)}) collective-permute-start(bf16[2,128,256]{1,2,0:T(8,128)(2,1)S(1)} %get-tuple-element.515), channel_id=1, source_target_pairs={{0,4},{1,5},{2,6},{3,7},{4,8},{5,9},{6,10},{7,11},{8,12},{9,13},{1... | collective-permute-start | bytes 393224 | tf_op jit(solution)/shard_map/while/body/eval_jaxpr/ppermute | solution.py:17
  49.1 4.8 %collective-permute-start = (bf16[2,128,256]{1,2,0:T(8,128)(2,1)S(1)}, bf16[2,128,256]{1,2,0:T(8,128)(2,1)S(1)}, u32[]{:S(2)}, u32[]{:S(2)}) collective-permute-start(bf16[2,128,256]{1,2,0:T(8,128)(2,1)S(1)} %get-tuple-element.515), channel_id=1, source_target_pairs={{0,4},{1,5},{2,6},{3,7},{4,8},{5,9},{6,10},{7,11},{8,12},{9,13},{1... | collective-permute-start | bytes 393224 | tf_op jit(solution)/shard_map/while/body/eval_jaxpr/ppermute | solution.py:17
  93.8 6.0 %copy-start.8 = (f32[2048]{0:T(1024)S(1)}, f32[2048]{0:T(1024)}, u32[]{:S(2)}) copy-start(f32[2048]{0:T(1024)} %param.23) | copy-start | bytes 24580
  98.8 1.0 copy-start.2
  251.9 4.9 %copy-start.7 = (f32[128,8]{0,1:T(8,128)S(1)}, f32[128,8]{0,1:T(8,128)}, u32[]{:S(2)}) copy-start(f32[128,8]{0,1:T(8,128)} %param.21) | copy-start | bytes 12292
  251.9 108.6 %all-to-all-start.1 = ((bf16[16,72,2048]{2,1,0:T(8,128)(2,1)}), bf16[16,72,2048]{2,1,0:T(8,128)(2,1)}, u32[]{:S(2)}, u32[]{:S(2)}) async-start(bf16[16,72,2048]{2,1,0:T(8,128)(2,1)} %bitcast.136), calls=%async_computation.1 | async-start | bytes 9437184 | tf_op jit(solution)/shard_map/all_to_all | solution.py:135
  372.4 22.3 %copy-start.3 = (f32[128,2048]{1,0:T(8,128)S(1)}, f32[128,2048]{1,0:T(8,128)}, u32[]{:S(2)}) copy-start(f32[128,2048]{1,0:T(8,128)} %copy-done.2) | copy-start | bytes 3145732
  394.7 5.5 %copy-start.1 = (bf16[1,768,2048]{2,1,0:T(8,128)(2,1)S(1)}, bf16[1,768,2048]{2,1,0:T(8,128)(2,1)}, u32[]{:S(2)}) copy-start(bf16[1,768,2048]{2,1,0:T(8,128)(2,1)} %param.25) | copy-start | bytes 9437188
Sparse Core Ops, SparseCore 0:
  10.2 83.6 all-gather.1
where the time goes:
time: 408 us; the launch traced here: 407 us
  waiting for transfers between devices  146 us (36%)
  blocking collectives  112 us (27%)
  local copies, waits for them, and re-layouts  68.9 us (17%)
  matrix products  36.1 us (9%)
  between operations  15 us (4%)
  other arithmetic  14.8 us (4%)
  loops' own time  8.25 us (2%)
  starting transfers between devices  6.42 us (2%)
    all_to_all x1, blocking collectives, local(): lax.all_to_all(outgoing, 'ctx', split_axis=0, concat_axis=0, tiled=True)  112 us
    all_to_all x1, waiting for transfers between devices, local(): lax.all_to_all(result, 'ctx', split_axis=0, concat_axis=0, tiled=True)  104 us
    all_gather x1, waiting for transfers between devices, local(): full_weight = lax.all_gather(out_weight, 'ctx', axis=1, tiled=True)  25.8 us
    scatter x1, local copies, waits for them, and re-layouts, local(): outgoing = jnp.zeros((experts * capacity, D), jnp.bfloat16).at[target].se...  23.8 us
    slice x1, local copies, waits for them, and re-layouts, local(): gathered[:, slot].astype(jnp.float32)  22.3 us
    ppermute x3, waiting for transfers between devices, shifted(): lax.ppermute(array, axis, [(i, (i + by) % devices) for i in range(devices)])  15.5 us
    gather x1, local copies, waits for them, and re-layouts, local(): returned.reshape(-1, D)[target].reshape(device_row_count, TOPK, D)  11.8 us
    dot_general x4, matrix products, update(): jnp.einsum('hqk,khd->hqd', weights.astype(jnp.bfloat16), local_value_bloc...  10 us
  transfers between devices with their start and end apart: 5, of which 5 were waited for; matrix products, arithmetic and copies ran while one was open for 8% of the time, Pallas kernels for 0%

commit v1 on v0

--- a/solution.py
+++ b/solution.py
@@ -35,7 +35,16 @@
     devices = lax.axis_size("ctx")
     cycle_length = devices // SEQS
     own_index = lax.axis_index("ctx")
-    full_weight = lax.all_gather(out_weight, "ctx", axis=1, tiled=True)
+    ways = lax.axis_size("ctx")
+    up = [(d, (d + 1) % ways) for d in range(ways)]
+    down = [(d, (d - 1) % ways) for d in range(ways)]
+    earlier, later = ([out_weight], [out_weight])
+    for _ in range(ways // 2):
+        earlier.append(lax.ppermute(earlier[-1], "ctx", up))
+    for _ in range((ways - 1) // 2):
+        later.append(lax.ppermute(later[-1], "ctx", down))
+    line = jnp.concatenate([*earlier[::-1], *later[1:]], axis=1)
+    full_weight = jnp.roll(line, (lax.axis_index("ctx") - ways // 2) * out_weight.shape[1], axis=1)
     query_position = block_order[own_index]
     query_head_rows = (
         queries.reshape(device_row_count, KEY_VALUE_HEADS, query_group_width, HEAD_SIZE)

time: 408 us -> 480 us (1.18); the launches traced: 407 us -> 471 us
  starting transfers between devices: 6.42 us -> 57.7 us
  local copies, waits for them, and re-layouts: 68.9 us -> 101 us
  between operations: 15 us -> 2.02 us
  waiting for transfers between devices: 146 us -> 141 us
    ppermute x0 -> x15, starting transfers between devices: none -> 51.1 us  [the longest x7 40.2 us: local(): later.append(lax.ppermute(later[-1], 'ctx', down))]
    ppermute x0 -> x15, waiting for transfers between devices: none -> 27.3 us  [the longest x7 14.7 us: local(): later.append(lax.ppermute(later[-1], 'ctx', down))]
    unnamed x25 -> x60, local copies, waits for them, and re-layouts: 5.92 us -> 33.2 us
    all_gather x1 -> x0, waiting for transfers between devices: 25.8 us -> none  [local(): full_weight = lax.all_gather(out_weight, 'ctx', axis=1, tiled=True)]
    ppermute x3, waiting for transfers between devices: 15.5 us -> 9.97 us  [shifted(): lax.ppermute(array, axis, [(i, (i + by) % devices) for i in range(devices)])]
  transfers between devices with their start and end apart: 5 -> 19, of which waited for: 5 -> 9; matrix products, arithmetic and copies ran while one was open for 8% -> 11% of each run, Pallas kernels for 0% -> 0%
where the time goes in v1:
time: 480 us; the launch traced here: 471 us
  waiting for transfers between devices  141 us (29%)
  blocking collectives  113 us (24%)
  local copies, waits for them, and re-layouts  101 us (21%)
  starting transfers between devices  57.7 us (12%)
  matrix products  33.4 us (7%)
  other arithmetic  15.5 us (3%)
  loops' own time  7.28 us (2%)
    all_to_all x1, blocking collectives, local(): lax.all_to_all(outgoing, 'ctx', split_axis=0, concat_axis=0, tiled=True)  113 us
    all_to_all x1, waiting for transfers between devices, local(): lax.all_to_all(result, 'ctx', split_axis=0, concat_axis=0, tiled=True)  104 us
    ppermute x7, starting transfers between devices, local(): later.append(lax.ppermute(later[-1], 'ctx', down))  40.2 us
    unnamed x60, local copies, waits for them, and re-layouts  33.2 us
    scatter x1, local copies, waits for them, and re-layouts, local(): outgoing = jnp.zeros((experts * capacity, D), jnp.bfloat16).at[target].se...  23.8 us
    slice x1, local copies, waits for them, and re-layouts, local(): gathered[:, slot].astype(jnp.float32)  21.7 us
    ppermute x7, waiting for transfers between devices, local(): later.append(lax.ppermute(later[-1], 'ctx', down))  14.7 us
    ppermute x8, waiting for transfers between devices, local(): earlier.append(lax.ppermute(earlier[-1], 'ctx', up))  12.6 us
  transfers between devices with their start and end apart: 19, of which 9 were waited for; matrix products, arithmetic and copies ran while one was open for 11% of the time, Pallas kernels for 0%

profile of v1, /device:TPU:13, one launch (start us, length us, event | category | flops | bytes accessed | tf_op | source)
XLA Modules:
  0.0 471.0 jit_solution(6025619554911358990)
XLA Ops:
  0.6 1.9 collective-permute-start.1
  2.5 6.4 %collective-permute-done.1 = bf16[2048,128]{1,0:T(8,128)(2,1)S(1)} collective-permute-done((bf16[2048,128]{1,0:T(8,128)(2,1)}, bf16[2048,128]{1,0:T(8,128)(2,1)S(1)}, u32[]{:S(2)}, u32[]{:S(2)}) %collective-permute-start.1) | collective-permute-done | bytes 524320 | tf_op jit(solution)/shard_map/ppermute | solution.py:43
  9.7 3.3 collective-permute-start.2
  13.0 6.2 %collective-permute-done.2 = bf16[2048,128]{1,0:T(8,128)(2,1)} collective-permute-done((bf16[2048,128]{1,0:T(8,128)(2,1)S(1)}, bf16[2048,128]{1,0:T(8,128)(2,1)}, u32[]{:S(2)}, u32[]{:S(2)}) %collective-permute-start.2) | collective-permute-done | bytes 524320 | tf_op jit(solution)/shard_map/ppermute | solution.py:43
  19.2 3.5 collective-permute-start.3
  22.7 1.2 dynamic_slice.17
  24.6 6.2 %collective-permute-start.10 = (bf16[2048,128]{1,0:T(8,128)(2,1)}, bf16[2048,128]{1,0:T(8,128)(2,1)}, u32[]{:S(2)}, u32[]{:S(2)}) collective-permute-start(bf16[2048,128]{1,0:T(8,128)(2,1)} %collective-permute-done.9), channel_id=1, source_target_pairs={{0,15},{1,0},{2,1},{3,2},{4,3},{5,4},{6,5},{7,6},{8,7},{9,8},{10,9... | collective-permute-start | bytes 1572872 | tf_op jit(solution)/shard_map/ppermute | solution.py:45
  30.8 1.9 collective-permute-start.4
  36.8 1.4 fusion.55
  39.4 7.3 %collective-permute-start.11 = (bf16[2048,128]{1,0:T(8,128)(2,1)}, bf16[2048,128]{1,0:T(8,128)(2,1)}, u32[]{:S(2)}, u32[]{:S(2)}) collective-permute-start(bf16[2048,128]{1,0:T(8,128)(2,1)} %collective-permute-done.10), channel_id=1, source_target_pairs={{0,15},{1,0},{2,1},{3,2},{4,3},{5,4},{6,5},{7,6},{8,7},{9,8},{10,9... | collective-permute-start | bytes 1572872 | tf_op jit(solution)/shard_map/ppermute | solution.py:45
  47.7 2.7 convolution_add_fusion.1
  50.4 3.8 collective-permute-done.11
  54.2 5.1 %collective-permute-start.12 = (bf16[2048,128]{1,0:T(8,128)(2,1)}, bf16[2048,128]{1,0:T(8,128)(2,1)}, u32[]{:S(2)}, u32[]{:S(2)}) collective-permute-start(bf16[2048,128]{1,0:T(8,128)(2,1)} %collective-permute-done.11), channel_id=1, source_target_pairs={{0,15},{1,0},{2,1},{3,2},{4,3},{5,4},{6,5},{7,6},{8,7},{9,8},{10,9... | collective-permute-start | bytes 1572872 | tf_op jit(solution)/shard_map/ppermute | solution.py:45
  59.4 38.0 %while.22 = (s32[]{:T(128)}, f32[2,1024,128]{2,1,0:T(8,128)}, f32[2,1024]{1,0:T(2,128)S(1)}, f32[2,1024]{1,0:T(2,128)S(1)}, bf16[2,128,256]{1,2,0:T(8,128)(2,1)}...) while((s32[]{:T(128)}, f32[2,1024,128]{2,1,0:T(8,128)}, ...), condition=%wide.region_7.8_spmd.clone, body=%wide.region_2.7_spmd.clone.sunk | while | flops 136719504 | bytes 7379506 | solution.py:106
  59.4 1.4 collective-permute-start
  60.7 1.3 dynamic_slice.27
  63.2 6.9 %collective-permute-done = bf16[2,128,256]{1,2,0:T(8,128)(2,1)S(1)} collective-permute-done((bf16[2,128,256]{1,2,0:T(8,128)(2,1)}, bf16[2,128,256]{1,2,0:T(8,128)(2,1)S(1)}, u32[]{:S(2)}, u32[]{:S(2)}) %collective-permute-start) | collective-permute-done | bytes 131104 | tf_op jit(solution)/shard_map/while/body/eval_jaxpr/ppermute | solution.py:17
  70.1 5.7 %conditional.3 = ((f32[2,1024,128]{2,1,0:T(8,128)}, f32[2,1024]{1,0:T(2,128)S(1)}, f32[2,1024]{1,0:T(2,128)S(1)})) conditional(s32[]{:T(128)} %convert_element_type.146, (f32[2,1024,128]{2,1,0:T(8,128)}, f32[2,1024]{1,0:T(2,128)S(1)}, f32[2,1024]{1,0:T(2,128)S(1)}) %tuple.77, (s32[]{:T(128)}, s32[128]{0:T(128)S(1)}, s32[]{:T(128)}, ...), branch_computations={%region_3.3_spmd, %region_4.6_spmd.clone} | conditional | flops 136718464 | bytes 6583872 | solution.py:98
  71.5 1.4 fusion.53
  73.2 2.7 convolution_add_fusion
  76.5 1.3 dynamic_slice.27
  79.0 1.5 collective-permute-done
  80.6 5.7 %conditional.3 = ((f32[2,1024,128]{2,1,0:T(8,128)}, f32[2,1024]{1,0:T(2,128)S(1)}, f32[2,1024]{1,0:T(2,128)S(1)})) conditional(s32[]{:T(128)} %convert_element_type.146, (f32[2,1024,128]{2,1,0:T(8,128)}, f32[2,1024]{1,0:T(2,128)S(1)}, f32[2,1024]{1,0:T(2,128)S(1)}) %tuple.77, (s32[]{:T(128)}, s32[128]{0:T(128)S(1)}, s32[]{:T(128)}, ...), branch_computations={%region_3.3_spmd, %region_4.6_spmd.clone} | conditional | flops 136718464 | bytes 6583872 | solution.py:98
  81.9 1.4 fusion.53
  83.6 2.7 convolution_add_fusion
  87.0 1.3 dynamic_slice.27
  89.5 1.5 collective-permute-done
  91.0 5.7 %conditional.3 = ((f32[2,1024,128]{2,1,0:T(8,128)}, f32[2,1024]{1,0:T(2,128)S(1)}, f32[2,1024]{1,0:T(2,128)S(1)})) conditional(s32[]{:T(128)} %convert_element_type.146, (f32[2,1024,128]{2,1,0:T(8,128)}, f32[2,1024]{1,0:T(2,128)S(1)}, f32[2,1024]{1,0:T(2,128)S(1)}) %tuple.77, (s32[]{:T(128)}, s32[128]{0:T(128)S(1)}, s32[]{:T(128)}, ...), branch_computations={%region_3.3_spmd, %region_4.6_spmd.clone} | conditional | flops 136718464 | bytes 6583872 | solution.py:98
  92.4 1.4 fusion.53
  94.0 2.7 convolution_add_fusion
  97.4 2.4 divide_convert_fusion
  100.1 1.4 copy.30
  102.4 4.5 reduce-window.6
  107.5 5.7 %collective-permute-start.13 = (bf16[2048,128]{1,0:T(8,128)(2,1)}, bf16[2048,128]{1,0:T(8,128)(2,1)S(1)}, u32[]{:S(2)}, u32[]{:S(2)}) collective-permute-start(bf16[2048,128]{1,0:T(8,128)(2,1)} %collective-permute-done.12), channel_id=1, source_target_pairs={{0,15},{1,0},{2,1},{3,2},{4,3},{5,4},{6,5},{7,6},{8,7},{9,8},{10,9... | collective-permute-start | bytes 1572872 | tf_op jit(solution)/shard_map/ppermute | solution.py:45
  113.3 6.9 %collective-permute-done.13 = bf16[2048,128]{1,0:T(8,128)(2,1)S(1)} collective-permute-done((bf16[2048,128]{1,0:T(8,128)(2,1)}, bf16[2048,128]{1,0:T(8,128)(2,1)S(1)}, u32[]{:S(2)}, u32[]{:S(2)}) %collective-permute-start.13) | collective-permute-done | bytes 524320 | tf_op jit(solution)/shard_map/ppermute | solution.py:45
  120.2 5.6 %collective-permute-start.14 = (bf16[2048,128]{1,0:T(8,128)(2,1)S(1)}, bf16[2048,128]{1,0:T(8,128)(2,1)S(1)}, u32[]{:S(2)}, u32[]{:S(2)}) collective-permute-start(bf16[2048,128]{1,0:T(8,128)(2,1)S(1)} %collective-permute-done.13), channel_id=1, source_target_pairs={{0,15},{1,0},{2,1},{3,2},{4,3},{5,4},{6,5},{7,6},{8,7},{9,8},{10,9... | collective-permute-start | bytes 1572872 | tf_op jit(solution)/shard_map/ppermute | solution.py:45
  125.8 3.9 collective-permute-done.14
  129.8 10.4 %collective-permute-start.15 = (bf16[2048,128]{1,0:T(8,128)(2,1)S(1)}, bf16[2048,128]{1,0:T(8,128)(2,1)S(1)}, u32[]{:S(2)}, u32[]{:S(2)}) collective-permute-start(bf16[2048,128]{1,0:T(8,128)(2,1)S(1)} %collective-permute-done.14), channel_id=1, source_target_pairs={{0,15},{1,0},{2,1},{3,2},{4,3},{5,4},{6,5},{7,6},{8,7},{9,8},{10,9... | collective-permute-start | bytes 1572872 | tf_op jit(solution)/shard_map/ppermute | solution.py:45
  140.5 1.2 constant_dynamic-update-slice_fusion.29
  141.7 1.2 constant_dynamic-update-slice_fusion.28
  142.9 1.2 constant_dynamic-update-slice_fusion.27
  144.2 1.2 constant_dynamic-update-slice_fusion.26
  145.4 1.2 constant_dynamic-update-slice_fusion.25
  146.6 1.2 constant_dynamic-update-slice_fusion.24
  147.8 1.2 constant_dynamic-update-slice_fusion.23
  149.1 1.2 constant_dynamic-update-slice_fusion.22
  150.3 1.2 constant_dynamic-update-slice_fusion.21
  151.5 1.2 constant_dynamic-update-slice_fusion.20
  152.8 1.2 constant_dynamic-update-slice_fusion.19
  157.4 1.2 constant_dynamic-update-slice_fusion.11
  158.6 1.2 constant_dynamic-update-slice_fusion.10
  159.8 1.2 constant_dynamic-update-slice_fusion.9
  161.5 1.2 constant_dynamic-update-slice_fusion.6
  162.7 1.2 constant_dynamic-update-slice_fusion.5
  167.0 1.5 multiply_reduce_fusion
  170.4 23.8 %scatter_custom_fusion = bf16[1152,2048]{1,0:T(8,128)(2,1)} fusion(s32[1024]{0:T(1024)S(1)} %bitcast.147, bf16[128,2048]{1,0:T(8,128)(2,1)} %multiply_convert_fusion, s32[1024]{0:T(1024)S(1)} %broadcast_clamp_fusion.1, bf16[]{:T(256)} %constant.152.clone.1), kind=kCustom, calls=%fused_computation.25 | custom fusion | bytes 4719104 | tf_op jit(solution)/shard_map/scatter | solution.py:132
  194.1 113.3 %all_to_all.10 = bf16[16,72,2048]{2,1,0:T(8,128)(2,1)S(1)} all-to-all(bf16[16,72,2048]{2,1,0:T(8,128)(2,1)} %bitcast.132), channel_id=1, replica_groups=mesh['groups'=2,'ctx'=16] {'ctx'}, dimensions={0} | all-to-all | bytes 9437184 | tf_op jit(solution)/shard_map/all_to_all | solution.py:135
  307.5 9.7 %fusion.12 = f32[1152,1536]{1,0:T(8,128)S(1)} fusion(bf16[1152,2048]{1,0:T(8,128)(2,1)S(1)} %bitcast.136, bf16[1,2048,1536]{2,1,0:T(8,128)(2,1)} %param.24), kind=kOutput, calls=%fused_computation.23 | convolution fusion | flops 7247757312 | bytes 18087936 | tf_op jit(solution)/shard_map/dot_general | solution.py:137
  317.2 5.7 %convolution_convert_fusion = bf16[1152,2048]{1,0:T(8,128)(2,1)} fusion(bf16[1,768,2048]{2,1,0:T(8,128)(2,1)S(1)} %copy-done, f32[1152,1536]{1,0:T(8,128)S(1)} %fusion.12), kind=kOutput, calls=%fused_computation.22 | convolution fusion | flops 3631546368 | bytes 14942208 | tf_op jit(solution)/shard_map/dot_general | solution.py:140
  322.9 5.2 %all-to-all-start.1 = ((bf16[16,72,2048]{2,1,0:T(8,128)(2,1)}), bf16[16,72,2048]{2,1,0:T(8,128)(2,1)}, u32[]{:S(2)}, u32[]{:S(2)}) async-start(bf16[16,72,2048]{2,1,0:T(8,128)(2,1)} %bitcast.135), calls=%async_computation.1 | async-start | bytes 9437184 | tf_op jit(solution)/shard_map/all_to_all | solution.py:144
  328.1 103.6 %all-to-all-done.1 = bf16[16,72,2048]{2,1,0:T(8,128)(2,1)} async-done(((bf16[16,72,2048]{2,1,0:T(8,128)(2,1)}), bf16[16,72,2048]{2,1,0:T(8,128)(2,1)}, u32[]{:S(2)}, u32[]{:S(2)}) %all-to-all-start.1) | async-done | bytes 4718624 | tf_op jit(solution)/shard_map/all_to_all | solution.py:144
  431.8 11.8 %gather_fusion = bf16[1024,2048]{1,0:T(8,128)(2,1)} fusion(bf16[1152,2048]{1,0:T(8,128)(2,1)} %bitcast.20, s32[1024]{0:T(1024)S(1)} %broadcast_clamp_fusion), kind=kCustom, calls=%fused_computation.1 | custom fusion | bytes 8392704 | tf_op jit(solution)/shard_map/gather | solution.py:145
  443.6 21.7 %fusion.54 = (bf16[128,1,2048]{2,1,0:T(2,128)(2,1)S(1)}, bf16[128,1,2048]{2,1,0:T(2,128)(2,1)S(1)}, bf16[128,1,2048]{2,1,0:T(2,128)(2,1)S(1)}, bf16[128,1,2048]{...) fusion(bf16[128,8,2048]{2,1,0:T(8,128)(2,1)} %bitcast.129), kind=kLoop, calls=%fused_computation.147 | loop fusion | bytes 8388608 | tf_op jit(solution)/shard_map/slice | solution.py:149
  465.3 5.5 %fusion.26 = bf16[128,2048]{1,0:T(8,128)(2,1)} fusion(f32[128,2048]{1,0:T(8,128)S(1)} %copy-done.3, bf16[128,1,2048]{2,1,0:T(2,128)(2,1)S(1)} %get-tuple-element.415, bf16[128,1,2048]{2,1,0:T(2,128)(2,1)S(1)} %get-tuple-element.409, bf16[128,1,2048]{2,1,0:T(2,128)(2,1)S(1)} %get-tuple-element.410, bf16[128,1,2048]{2,1,0:T(2,128)(2,1)S(1)} %get-tuple-element.411, ...), kind=kLoop, calls=%fused_computation.38 | loop fusion | flops 6553600 | bytes 5771264 | tf_op jit(solution)/shard_map/convert_element_type | solution.py:150
  (128 shorter events, 21.1 us)
Async XLA Ops:
  0.6 316.5 %copy-start = (bf16[1,768,2048]{2,1,0:T(8,128)(2,1)S(1)}, bf16[1,768,2048]{2,1,0:T(8,128)(2,1)}, u32[]{:S(2)}) copy-start(bf16[1,768,2048]{2,1,0:T(8,128)(2,1)} %param.25) | copy-start | bytes 9437188
  0.6 8.3 %collective-permute-start.1 = (bf16[2048,128]{1,0:T(8,128)(2,1)}, bf16[2048,128]{1,0:T(8,128)(2,1)S(1)}, u32[]{:S(2)}, u32[]{:S(2)}) collective-permute-start(bf16[2048,128]{1,0:T(8,128)(2,1)} %param.22), channel_id=1, source_target_pairs={{0,1},{1,2},{2,3},{3,4},{4,5},{5,6},{6,7},{7,8},{8,9},{9,10},{10,1... | collective-permute-start | bytes 1572872 | tf_op jit(solution)/shard_map/ppermute | solution.py:43
  8.9 0.8 copy-start.5
  9.7 9.4 %collective-permute-start.2 = (bf16[2048,128]{1,0:T(8,128)(2,1)S(1)}, bf16[2048,128]{1,0:T(8,128)(2,1)}, u32[]{:S(2)}, u32[]{:S(2)}) collective-permute-start(bf16[2048,128]{1,0:T(8,128)(2,1)S(1)} %collective-permute-done.1), channel_id=1, source_target_pairs={{0,1},{1,2},{2,3},{3,4},{4,5},{5,6},{6,7},{7,8},{8,9},{9,10},{10,1... | collective-permute-start | bytes 1572872 | tf_op jit(solution)/shard_map/ppermute | solution.py:43
  13.0 11.5 %collective-permute-start.9 = (bf16[2048,128]{1,0:T(8,128)(2,1)}, bf16[2048,128]{1,0:T(8,128)(2,1)}, u32[]{:S(2)}, u32[]{:S(2)}) collective-permute-start(bf16[2048,128]{1,0:T(8,128)(2,1)} %param.22), channel_id=1, source_target_pairs={{0,15},{1,0},{2,1},{3,2},{4,3},{5,4},{6,5},{7,6},{8,7},{9,8},{10,9... | collective-permute-start | bytes 1572872 | tf_op jit(solution)/shard_map/ppermute | solution.py:45
  19.2 11.6 %collective-permute-start.3 = (bf16[2048,128]{1,0:T(8,128)(2,1)}, bf16[2048,128]{1,0:T(8,128)(2,1)}, u32[]{:S(2)}, u32[]{:S(2)}) collective-permute-start(bf16[2048,128]{1,0:T(8,128)(2,1)} %collective-permute-done.2), channel_id=1, source_target_pairs={{0,1},{1,2},{2,3},{3,4},{4,5},{5,6},{6,7},{7,8},{8,9},{9,10},{10,1... | collective-permute-start | bytes 1572872 | tf_op jit(solution)/shard_map/ppermute | solution.py:43
  24.6 14.8 %collective-permute-start.10 = (bf16[2048,128]{1,0:T(8,128)(2,1)}, bf16[2048,128]{1,0:T(8,128)(2,1)}, u32[]{:S(2)}, u32[]{:S(2)}) collective-permute-start(bf16[2048,128]{1,0:T(8,128)(2,1)} %collective-permute-done.9), channel_id=1, source_target_pairs={{0,15},{1,0},{2,1},{3,2},{4,3},{5,4},{6,5},{7,6},{8,7},{9,8},{10,9... | collective-permute-start | bytes 1572872 | tf_op jit(solution)/shard_map/ppermute | solution.py:45
  30.8 15.9 %collective-permute-start.4 = (bf16[2048,128]{1,0:T(8,128)(2,1)}, bf16[2048,128]{1,0:T(8,128)(2,1)}, u32[]{:S(2)}, u32[]{:S(2)}) collective-permute-start(bf16[2048,128]{1,0:T(8,128)(2,1)} %collective-permute-done.3), channel_id=1, source_target_pairs={{0,1},{1,2},{2,3},{3,4},{4,5},{5,6},{6,7},{7,8},{8,9},{9,10},{10,1... | collective-permute-start | bytes 1572872 | tf_op jit(solution)/shard_map/ppermute | solution.py:43
  38.2 1.0 copy-start.1
  39.4 14.8 %collective-permute-start.11 = (bf16[2048,128]{1,0:T(8,128)(2,1)}, bf16[2048,128]{1,0:T(8,128)(2,1)}, u32[]{:S(2)}, u32[]{:S(2)}) collective-permute-start(bf16[2048,128]{1,0:T(8,128)(2,1)} %collective-permute-done.10), channel_id=1, source_target_pairs={{0,15},{1,0},{2,1},{3,2},{4,3},{5,4},{6,5},{7,6},{8,7},{9,8},{10,9... | collective-permute-start | bytes 1572872 | tf_op jit(solution)/shard_map/ppermute | solution.py:45
  46.7 12.7 %collective-permute-start.5 = (bf16[2048,128]{1,0:T(8,128)(2,1)}, bf16[2048,128]{1,0:T(8,128)(2,1)}, u32[]{:S(2)}, u32[]{:S(2)}) collective-permute-start(bf16[2048,128]{1,0:T(8,128)(2,1)} %collective-permute-done.4), channel_id=1, source_target_pairs={{0,1},{1,2},{2,3},{3,4},{4,5},{5,6},{6,7},{7,8},{8,9},{9,10},{10,1... | collective-permute-start | bytes 1572872 | tf_op jit(solution)/shard_map/ppermute | solution.py:43
  54.2 53.2 %collective-permute-start.12 = (bf16[2048,128]{1,0:T(8,128)(2,1)}, bf16[2048,128]{1,0:T(8,128)(2,1)}, u32[]{:S(2)}, u32[]{:S(2)}) collective-permute-start(bf16[2048,128]{1,0:T(8,128)(2,1)} %collective-permute-done.11), channel_id=1, source_target_pairs={{0,15},{1,0},{2,1},{3,2},{4,3},{5,4},{6,5},{7,6},{8,7},{9,8},{10,9... | collective-permute-start | bytes 1572872 | tf_op jit(solution)/shard_map/ppermute | solution.py:45
  59.4 53.8 %collective-permute-start.6 = (bf16[2048,128]{1,0:T(8,128)(2,1)}, bf16[2048,128]{1,0:T(8,128)(2,1)}, u32[]{:S(2)}, u32[]{:S(2)}) collective-permute-start(bf16[2048,128]{1,0:T(8,128)(2,1)} %collective-permute-done.5), channel_id=1, source_target_pairs={{0,1},{1,2},{2,3},{3,4},{4,5},{5,6},{6,7},{7,8},{8,9},{9,10},{10,1... | collective-permute-start | bytes 1572872 | tf_op jit(solution)/shard_map/ppermute | solution.py:43
  59.4 40.4 %copy-start.9 = (s32[128,8]{0,1:T(8,128)S(1)}, s32[128,8]{0,1:T(8,128)}, u32[]{:S(2)}) copy-start(s32[128,8]{0,1:T(8,128)} %param.20) | copy-start | bytes 12292
  59.4 10.8 %collective-permute-start = (bf16[2,128,256]{1,2,0:T(8,128)(2,1)}, bf16[2,128,256]{1,2,0:T(8,128)(2,1)S(1)}, u32[]{:S(2)}, u32[]{:S(2)}) collective-permute-start(bf16[2,128,256]{1,2,0:T(8,128)(2,1)} %get-tuple-element.515), channel_id=1, source_target_pairs={{0,4},{1,5},{2,6},{3,7},{4,8},{5,9},{6,10},{7,11},{8,12},{9,13},{1... | collective-permute-start | bytes 393224 | tf_op jit(solution)/shard_map/while/body/eval_jaxpr/ppermute | solution.py:17
  76.5 4.0 collective-permute-start
  87.0 4.0 collective-permute-start
  107.4 53.6 %copy-start.6 = (bf16[2048,128]{1,0:T(8,128)(2,1)S(1)}, bf16[2048,128]{1,0:T(8,128)(2,1)}, u32[]{:S(2)}) copy-start(bf16[2048,128]{1,0:T(8,128)(2,1)} %copy-done.5) | copy-start | bytes 1572868
  107.4 53.8 %copy-start.4 = (bf16[2048,128]{1,0:T(8,128)(2,1)S(1)}, bf16[2048,128]{1,0:T(8,128)(2,1)}, u32[]{:S(2)}) copy-start(bf16[2048,128]{1,0:T(8,128)(2,1)} %param.22) | copy-start | bytes 1572868
  107.5 12.7 %collective-permute-start.13 = (bf16[2048,128]{1,0:T(8,128)(2,1)}, bf16[2048,128]{1,0:T(8,128)(2,1)S(1)}, u32[]{:S(2)}, u32[]{:S(2)}) collective-permute-start(bf16[2048,128]{1,0:T(8,128)(2,1)} %collective-permute-done.12), channel_id=1, source_target_pairs={{0,15},{1,0},{2,1},{3,2},{4,3},{5,4},{6,5},{7,6},{8,7},{9,8},{10,9... | collective-permute-start | bytes 1572872 | tf_op jit(solution)/shard_map/ppermute | solution.py:45
  113.1 12.6 %collective-permute-start.7 = (bf16[2048,128]{1,0:T(8,128)(2,1)}, bf16[2048,128]{1,0:T(8,128)(2,1)S(1)}, u32[]{:S(2)}, u32[]{:S(2)}) collective-permute-start(bf16[2048,128]{1,0:T(8,128)(2,1)} %collective-permute-done.6), channel_id=1, source_target_pairs={{0,1},{1,2},{2,3},{3,4},{4,5},{5,6},{6,7},{7,8},{8,9},{9,10},{10,1... | collective-permute-start | bytes 1572872 | tf_op jit(solution)/shard_map/ppermute | solution.py:43
  120.2 9.6 %collective-permute-start.14 = (bf16[2048,128]{1,0:T(8,128)(2,1)S(1)}, bf16[2048,128]{1,0:T(8,128)(2,1)S(1)}, u32[]{:S(2)}, u32[]{:S(2)}) collective-permute-start(bf16[2048,128]{1,0:T(8,128)(2,1)S(1)} %collective-permute-done.13), channel_id=1, source_target_pairs={{0,15},{1,0},{2,1},{3,2},{4,3},{5,4},{6,5},{7,6},{8,7},{9,8},{10,9... | collective-permute-start | bytes 1572872 | tf_op jit(solution)/shard_map/ppermute | solution.py:45
  125.8 14.4 %collective-permute-start.8 = (bf16[2048,128]{1,0:T(8,128)(2,1)S(1)}, bf16[2048,128]{1,0:T(8,128)(2,1)S(1)}, u32[]{:S(2)}, u32[]{:S(2)}) collective-permute-start(bf16[2048,128]{1,0:T(8,128)(2,1)S(1)} %collective-permute-done.7), channel_id=1, source_target_pairs={{0,1},{1,2},{2,3},{3,4},{4,5},{5,6},{6,7},{7,8},{8,9},{9,10},{10,1... | collective-permute-start | bytes 1572872 | tf_op jit(solution)/shard_map/ppermute | solution.py:43
  125.8 41.1 %copy-start.7 = (bf16[16,8,16,128]{3,1,2,0:T(8,128)(2,1)S(1)}, bf16[16,8,16,128]{3,1,2,0:T(8,128)(2,1)}, u32[]{:S(2)}) copy-start(bf16[16,8,16,128]{3,1,2,0:T(8,128)(2,1)} %copy.97) | copy-start | bytes 1572868
  125.8 41.1 %copy-start.8 = (bf16[128,2048]{1,0:T(8,128)(2,1)S(1)}, bf16[128,2048]{1,0:T(8,128)(2,1)}, u32[]{:S(2)}) copy-start(bf16[128,2048]{1,0:T(8,128)(2,1)} %param.15) | copy-start | bytes 1572868
  129.8 24.6 %collective-permute-start.15 = (bf16[2048,128]{1,0:T(8,128)(2,1)S(1)}, bf16[2048,128]{1,0:T(8,128)(2,1)S(1)}, u32[]{:S(2)}, u32[]{:S(2)}) collective-permute-start(bf16[2048,128]{1,0:T(8,128)(2,1)S(1)} %collective-permute-done.14), channel_id=1, source_target_pairs={{0,15},{1,0},{2,1},{3,2},{4,3},{5,4},{6,5},{7,6},{8,7},{9,8},{10,9... | collective-permute-start | bytes 1572872 | tf_op jit(solution)/shard_map/ppermute | solution.py:45
  150.3 19.1 %copy-start.11 = (f32[2048]{0:T(1024)S(1)}, f32[2048]{0:T(1024)}, u32[]{:S(2)}) copy-start(f32[2048]{0:T(1024)} %param.23) | copy-start | bytes 24580
  168.5 1.0 copy-start.2
  317.2 10.9 %copy-start.10 = (f32[128,8]{0,1:T(8,128)S(1)}, f32[128,8]{0,1:T(8,128)}, u32[]{:S(2)}) copy-start(f32[128,8]{0,1:T(8,128)} %param.21) | copy-start | bytes 12292
  322.9 108.9 %all-to-all-start.1 = ((bf16[16,72,2048]{2,1,0:T(8,128)(2,1)}), bf16[16,72,2048]{2,1,0:T(8,128)(2,1)}, u32[]{:S(2)}, u32[]{:S(2)}) async-start(bf16[16,72,2048]{2,1,0:T(8,128)(2,1)} %bitcast.135), calls=%async_computation.1 | async-start | bytes 9437184 | tf_op jit(solution)/shard_map/all_to_all | solution.py:144
  443.6 21.7 %copy-start.3 = (f32[128,2048]{1,0:T(8,128)S(1)}, f32[128,2048]{1,0:T(8,128)}, u32[]{:S(2)}) copy-start(f32[128,2048]{1,0:T(8,128)} %copy-done.2) | copy-start | bytes 3145732
